TPU v7x, 32 devices: a whole 2x2x4 slice. The times are simulated.
32 devices in a mesh: gx: 4 (over y, x), gy: 2 (over core), gz: 4 (over z).
Axes of the slice: x: 2, y: 2, z: 4, core: 2. Of those that a mesh axis runs over, the one named last changes fastest.
Arguments:
- correction: float32 [64, 64, 512], P('gz', 'gx', 'gy'), may hold values from -6 to 6
- residual: float32 [64, 64, 512], P('gz', 'gx', 'gy'), may hold values from -4 to 6
- state: float32 [64, 64, 512], P('gz', 'gx', 'gy'), may hold values from -1 to 1
- spacing_level: int32 [64], replicated, may hold values from 0 to 3
- line_colour: int32 [64, 512], P('gx', 'gy'), may hold values from 0 to 1
Outputs:
- smoothed: float32 [64, 64, 512], P('gz', 'gx', 'gy')
All inputs are finite; a program needn't handle non-finite values.
Results may differ from a plain program's by a relative error of at most 0.0003.
Values sent between devices are 32-bit elements; how exact they have to be, the bound alone decides.
A program may use at most 64 MiB of HBM per device.

v0:
```python
import jax
import jax.numpy as jnp
from jax import lax
from jax.sharding import PartitionSpec as P

coef_z = 1000.0
coef_x = 0.3
coef_y = 0.2
bratu_lambda = 0.2


def extended(block, sides, width):
    for axis, dim in sides:
        count = lax.axis_size(axis)
        forward = [(i, i + 1) for i in range(count - 1)]
        backward = [(target, source) for source, target in forward]
        low = lax.ppermute(
            lax.slice_in_dim(block, block.shape[dim] - width, None, axis=dim), axis, forward
        )
        high = lax.ppermute(lax.slice_in_dim(block, 0, width, axis=dim), axis, backward)
        block = jnp.concatenate([low, block, high], axis=dim)
    return block


def face_coupling(spacing_level):
    spacing_cells = 0.8 * jnp.power(1.3, spacing_level.astype(jnp.float32))
    inner_faces = coef_z * 2.0 / (spacing_cells[:-1] + spacing_cells[1:])
    nothing = jnp.zeros((1,), jnp.float32)
    face_low = jnp.concatenate([nothing, inner_faces])
    face_high = jnp.concatenate([inner_faces, nothing])
    return (spacing_cells, face_low, face_high)


def move_rows(values, stride, filler):
    length = values.shape[0]
    padding = jnp.full((abs(stride),) + values.shape[1:], filler, values.dtype)
    if stride > 0:
        return jnp.concatenate([padding, values[: length - stride]], 0)
    return jnp.concatenate([values[-stride:], padding], 0)


def factor_local(below_coef, centre, above_coef):
    length = centre.shape[0]
    sections = []
    stride = 1
    while stride < length:
        before_low = move_rows(below_coef, stride, 0.0)
        before_mid = move_rows(centre, stride, 1.0)
        before_high = move_rows(above_coef, stride, 0.0)
        beyond_low = move_rows(below_coef, -stride, 0.0)
        beyond_mid = move_rows(centre, -stride, 1.0)
        beyond_high = move_rows(above_coef, -stride, 0.0)
        weight_low = -below_coef / before_mid
        weight_high = -above_coef / beyond_mid
        centre = centre + weight_low * before_high + weight_high * beyond_low
        below_coef = weight_low * before_low
        above_coef = weight_high * beyond_high
        sections.append((weight_low, weight_high))
        stride = stride * 2
    return (sections, centre)


def apply_local(source, sections, centre):
    stride = 1
    for weight_low, weight_high in sections:
        source = (
            source
            + weight_low * move_rows(source, stride, 0.0)
            + weight_high * move_rows(source, -stride, 0.0)
        )
        stride = stride * 2
    return source / centre


def on_device(correction, residual, state, spacing_level, line_colour):
    depth = correction.shape[0]
    device_place = lax.axis_index("gz")
    spacing_all, face_low_all, face_high_all = face_coupling(spacing_level)
    offset_rows = device_place * depth
    spacing_cells = lax.dynamic_slice_in_dim(spacing_all, offset_rows, depth)
    face_low = lax.dynamic_slice_in_dim(face_low_all, offset_rows, depth)
    face_high = lax.dynamic_slice_in_dim(face_high_all, offset_rows, depth)
    column = spacing_cells[:, None, None]
    centre = (face_low + face_high)[:, None, None] + column * (
        2.0 * coef_x + 2.0 * coef_y - bratu_lambda * jnp.exp(state)
    )
    line_shape = centre.shape
    row_column = jnp.arange(depth)[:, None, None]
    edge_rows = (row_column == 0) | (row_column == depth - 1)
    low_full = jnp.broadcast_to((-face_low)[:, None, None], line_shape)
    high_full = jnp.broadcast_to((-face_high)[:, None, None], line_shape)
    inner_low = jnp.where((row_column <= 1) | (row_column == depth - 1), 0.0, low_full)
    inner_high = jnp.where((row_column >= depth - 2) | (row_column == 0), 0.0, high_full)
    inner_centre = jnp.where(edge_rows, 1.0, centre)
    sections_local, centre_local = factor_local(inner_low, inner_centre, inner_high)
    from_first = apply_local(
        jnp.where(row_column == 1, -low_full, 0.0), sections_local, centre_local
    )
    from_last = apply_local(
        jnp.where(row_column == depth - 2, -high_full, 0.0), sections_local, centre_local
    )
    first_low = low_full[0]
    first_mid = centre[0] + high_full[0] * from_first[1]
    first_high = high_full[0] * from_last[1]
    last_low = low_full[depth - 1] * from_first[depth - 2]
    last_mid = centre[depth - 1] + low_full[depth - 1] * from_last[depth - 2]
    last_high = high_full[depth - 1]
    coupled = jnp.stack(
        [
            jnp.stack([first_low, last_low], 0),
            jnp.stack([first_mid, last_mid], 0),
            jnp.stack([first_high, last_high], 0),
        ],
        0,
    )
    gathered = lax.all_gather(coupled, "gz", axis=1, tiled=True)
    sections_reduced, centre_reduced = factor_local(gathered[0], gathered[1], gathered[2])
    iterate = correction
    for colour in range(2):
        padded = extended(iterate, (("gx", 1), ("gy", 2)), 1)
        beside = coef_x * (padded[:, 2:, 1:-1] + padded[:, :-2, 1:-1]) + coef_y * (
            padded[:, 1:-1, 2:] + padded[:, 1:-1, :-2]
        )
        source = column * (residual + beside)
        interior = apply_local(jnp.where(edge_rows, 0.0, source), sections_local, centre_local)
        first_source = source[0] - high_full[0] * interior[1]
        last_source = source[depth - 1] - low_full[depth - 1] * interior[depth - 2]
        source_pair = jnp.stack([first_source, last_source], 0)
        all_sources = lax.all_gather(source_pair, "gz", axis=0, tiled=True)
        solution = apply_local(all_sources, sections_reduced, centre_reduced)
        ends_value = lax.dynamic_slice_in_dim(solution, 2 * device_place, 2, 0)
        first_cell = ends_value[0]
        last_cell = ends_value[1]
        inside = interior + from_first * first_cell[None] + from_last * last_cell[None]
        solved = jnp.where(
            row_column == 0,
            first_cell[None],
            jnp.where(row_column == depth - 1, last_cell[None], inside),
        )
        iterate = jnp.where((line_colour == colour)[None], solved, iterate)
    return iterate


def solution(mesh):
    return jax.shard_map(
        on_device,
        mesh=mesh,
        in_specs=(
            P("gz", "gx", "gy"),
            P("gz", "gx", "gy"),
            P("gz", "gx", "gy"),
            P(),
            P("gx", "gy"),
        ),
        out_specs=P("gz", "gx", "gy"),
        check_vma=False,
    )
```

profile of v0, /device:TPU:12, one launch (start us, length us, event | category | flops | bytes accessed | tf_op | source)
XLA Modules:
  0.0 85.7 jit_solution(15522667361424550462)
XLA Ops:
  0.0 1.0 %fusion.55 = (f32[16,1,256]{2,1,0:T(1,128)S(1)}, f32[16,1,256]{2,1,0:T(1,128)S(1)}) fusion(f32[16,16,256]{2,1,0:T(8,128)} %param.5), kind=kLoop, calls=%fused_computation.170 | loop fusion | bytes 65536 | tf_op jit(solution)/shard_map/slice | solution.py:18
  1.0 3.3 %collective-permute-start = (f32[16,1,256]{2,1,0:T(1,128)S(1)}, f32[16,1,256]{2,1,0:T(1,128)S(1)}, u32[]{:S(2)}, u32[]{:S(2)}) collective-permute-start(f32[16,1,256]{2,1,0:T(1,128)S(1)} %get-tuple-element.94), channel_id=1, source_target_pairs={{8,0},{16,8},{24,16},{9,1},{17,9},{25,17},{10,2},{18,10},{26,18},{... | collective-permute-start | bytes 49160 | tf_op jit(solution)/shard_map/ppermute | solution.py:20
  4.3 2.5 %collective-permute-start.1 = (f32[16,1,256]{2,1,0:T(1,128)S(1)}, f32[16,1,256]{2,1,0:T(1,128)S(1)}, u32[]{:S(2)}, u32[]{:S(2)}) collective-permute-start(f32[16,1,256]{2,1,0:T(1,128)S(1)} %get-tuple-element.93), channel_id=1, source_target_pairs={{0,8},{8,16},{16,24},{1,9},{9,17},{17,25},{2,10},{10,18},{18,26},{... | collective-permute-start | bytes 49160 | tf_op jit(solution)/shard_map/ppermute | solution.py:17
  6.9 0.6 copy-done.4
  7.6 0.1 pad_maximum_fusion.22
  7.7 0.1 fusion.41
  7.9 0.1 broadcast_select_fusion.1
  8.0 0.1 broadcast_select_fusion
  8.2 0.6 fusion.83
  8.8 0.6 fusion.84
  9.5 1.4 %collective-permute-done.1 = f32[16,1,256]{2,1,0:T(1,128)S(1)} collective-permute-done((f32[16,1,256]{2,1,0:T(1,128)S(1)}, f32[16,1,256]{2,1,0:T(1,128)S(1)}, u32[]{:S(2)}, u32[]{:S(2)}) %collective-permute-start.1) | collective-permute-done | bytes 16416 | tf_op jit(solution)/shard_map/ppermute | solution.py:17
  11.0 0.1 fusion.44
  11.1 1.4 %collective-permute-start.2 = (f32[16,18,1]{2,1,0:T(8,128)S(1)}, f32[16,18,1]{2,1,0:T(8,128)S(1)}, u32[]{:S(2)}, u32[]{:S(2)}) collective-permute-start(f32[16,18,1]{2,1,0:T(8,128)S(1)} %get-tuple-element.63), channel_id=1, source_target_pairs={{4,0},{5,1},{6,2},{7,3},{12,8},{13,9},{14,10},{15,11},{20,16},{21,... | collective-permute-start | bytes 3464 | tf_op jit(solution)/shard_map/ppermute | solution.py:20
  12.5 3.0 %collective-permute-start.3 = (f32[16,18,1]{2,1,0:T(8,128)S(1)}, f32[16,18,1]{2,1,0:T(8,128)S(1)}, u32[]{:S(2)}, u32[]{:S(2)}) collective-permute-start(f32[16,18,1]{2,1,0:T(8,128)S(1)} %get-tuple-element.64), channel_id=1, source_target_pairs={{0,4},{1,5},{2,6},{3,7},{8,12},{9,13},{10,14},{11,15},{16,20},{17,... | collective-permute-start | bytes 3464 | tf_op jit(solution)/shard_map/ppermute | solution.py:17
  15.6 0.1 dynamic_slice.15
  15.7 0.9 %collective-permute-done.3 = f32[16,18,1]{2,1,0:T(8,128)S(1)} collective-permute-done((f32[16,18,1]{2,1,0:T(8,128)S(1)}, f32[16,18,1]{2,1,0:T(8,128)S(1)}, u32[]{:S(2)}, u32[]{:S(2)}) %collective-permute-start.3) | collective-permute-done | bytes 1184 | tf_op jit(solution)/shard_map/ppermute | solution.py:17
  16.6 0.4 broadcast_select_fusion.6
  17.1 0.2 broadcast_select_fusion.2
  17.3 0.2 multiply_add_fusion.5
  17.7 0.3 multiply_add_fusion.7
  18.1 0.1 multiply_add_fusion.12
  18.4 0.5 multiply_add_fusion.13
  19.1 0.3 multiply_add_fusion.11
  19.5 0.3 add_divide_fusion.2
  19.8 1.2 %slice_multiply_fusion.5 = (f32[1,16,256]{2,1,0:T(8,128)S(1)}, f32[1,16,256]{2,1,0:T(8,128)S(1)}, f32[1,16,256]{2,1,0:T(8,128)S(1)}, f32[1,16,256]{2,1,0:T(8,128)S(1)}) fusion(f32[16,16,256]{2,1,0:T(8,128)S(1)} %get-tuple-element.36, f32[]{:T(128)} %bitcast.1, f32[]{:T(128)} %bitcast, f32[16,16,256]{2,1,0:T(8,128)S(1)} %get-tuple-element.158, ...), kind=kLoop, calls=%fused_computation.138 | loop fusion | flops 24576 | bytes 163848 | tf_op jit(solution)/shard_map/mul | solution.py:105
  21.1 0.7 pad_bitcast_fusion.1
  21.7 0.6 pad_bitcast_fusion
  22.4 15.6 %all_gather.10 = f32[3,8,16,256]{3,2,1,0:T(8,128)S(1)} all-gather(f32[3,2,16,256]{3,2,1,0:T(8,128)S(1)} %pad_maximum_fusion.18), channel_id=1, replica_groups=mesh['gx'=4,'gy'=2,'gz'=4] {'gz'}, dimensions={1}, use_global_device_ids=true | all-gather | bytes 491520 | tf_op jit(solution)/shard_map/all_gather | solution.py:116
  38.1 0.2 add_divide_fusion.3
  38.3 1.2 %fusion.35 = (f32[1,16,256]{2,1,0:T(8,128)S(1)}, f32[1,16,256]{2,1,0:T(8,128)S(1)}) fusion(f32[16,16,256]{2,1,0:T(8,128)S(1)} %add_divide_fusion.3, f32[16,16,256]{2,1,0:T(8,128)S(1)} %get-tuple-element.29, f32[]{:T(128)} %bitcast, f32[]{:T(128)} %bitcast.1), kind=kLoop, calls=%fused_computation.142 | loop fusion | flops 16384 | bytes 98312 | tf_op jit(solution)/shard_map/sub | solution.py:126
  39.5 13.5 %all_gather.9 = f32[8,16,256]{2,1,0:T(8,128)S(1)} all-gather(f32[2,16,256]{2,1,0:T(8,128)S(1)} %pad_maximum_fusion.19), channel_id=1, replica_groups=mesh['gx'=4,'gy'=2,'gz'=4] {'gz'}, dimensions={0}, use_global_device_ids=true | all-gather | bytes 163840 | tf_op jit(solution)/shard_map/all_gather | solution.py:129
  53.4 0.1 multiply_add_fusion.20
  53.7 0.1 select_select_fusion.1
  53.8 2.9 %collective-permute-start.4 = (f32[16,1,256]{2,1,0:T(1,128)S(1)}, f32[16,1,256]{2,1,0:T(1,128)S(1)}, u32[]{:S(2)}, u32[]{:S(2)}) collective-permute-start(f32[16,1,256]{2,1,0:T(1,128)S(1)} %get-tuple-element.74), channel_id=1, source_target_pairs={{8,0},{16,8},{24,16},{9,1},{17,9},{25,17},{10,2},{18,10},{26,18},{... | collective-permute-start | bytes 49160 | tf_op jit(solution)/shard_map/ppermute | solution.py:20
  56.7 2.9 %collective-permute-start.5 = (f32[16,1,256]{2,1,0:T(1,128)S(1)}, f32[16,1,256]{2,1,0:T(1,128)S(1)}, u32[]{:S(2)}, u32[]{:S(2)}) collective-permute-start(f32[16,1,256]{2,1,0:T(1,128)S(1)} %get-tuple-element.73), channel_id=1, source_target_pairs={{0,8},{8,16},{16,24},{1,9},{9,17},{17,25},{2,10},{10,18},{18,26},{... | collective-permute-start | bytes 49160 | tf_op jit(solution)/shard_map/ppermute | solution.py:17
  59.7 3.6 %collective-permute-done.5 = f32[16,1,256]{2,1,0:T(1,128)S(1)} collective-permute-done((f32[16,1,256]{2,1,0:T(1,128)S(1)}, f32[16,1,256]{2,1,0:T(1,128)S(1)}, u32[]{:S(2)}, u32[]{:S(2)}) %collective-permute-start.5) | collective-permute-done | bytes 16416 | tf_op jit(solution)/shard_map/ppermute | solution.py:17
  63.3 0.1 fusion.43
  63.4 1.3 %collective-permute-start.6 = (f32[16,18,1]{2,1,0:T(8,128)S(1)}, f32[16,18,1]{2,1,0:T(8,128)S(1)}, u32[]{:S(2)}, u32[]{:S(2)}) collective-permute-start(f32[16,18,1]{2,1,0:T(8,128)S(1)} %get-tuple-element.55), channel_id=1, source_target_pairs={{4,0},{5,1},{6,2},{7,3},{12,8},{13,9},{14,10},{15,11},{20,16},{21,... | collective-permute-start | bytes 3464 | tf_op jit(solution)/shard_map/ppermute | solution.py:20
  64.7 3.0 %collective-permute-start.7 = (f32[16,18,1]{2,1,0:T(8,128)S(1)}, f32[16,18,1]{2,1,0:T(8,128)S(1)}, u32[]{:S(2)}, u32[]{:S(2)}) collective-permute-start(f32[16,18,1]{2,1,0:T(8,128)S(1)} %get-tuple-element.56), channel_id=1, source_target_pairs={{0,4},{1,5},{2,6},{3,7},{8,12},{9,13},{10,14},{11,15},{16,20},{17,... | collective-permute-start | bytes 3464 | tf_op jit(solution)/shard_map/ppermute | solution.py:17
  67.8 1.0 %collective-permute-done.7 = f32[16,18,1]{2,1,0:T(8,128)S(1)} collective-permute-done((f32[16,18,1]{2,1,0:T(8,128)S(1)}, f32[16,18,1]{2,1,0:T(8,128)S(1)}, u32[]{:S(2)}, u32[]{:S(2)}) %collective-permute-start.7) | collective-permute-done | bytes 1184 | tf_op jit(solution)/shard_map/ppermute | solution.py:17
  68.8 0.4 broadcast_select_fusion.5
  69.3 0.2 multiply_add_fusion.2
  69.5 0.1 multiply_add_fusion.1
  69.6 0.1 multiply_add_fusion
  69.8 0.2 add_divide_fusion
  70.0 1.2 %fusion.31 = (f32[1,16,256]{2,1,0:T(8,128)S(1)}, f32[1,16,256]{2,1,0:T(8,128)S(1)}) fusion(f32[16,16,256]{2,1,0:T(8,128)S(1)} %add_divide_fusion, f32[16,16,256]{2,1,0:T(8,128)S(1)} %get-tuple-element.6, f32[]{:T(128)} %bitcast, f32[]{:T(128)} %bitcast.1), kind=kLoop, calls=%fused_computation.130 | loop fusion | flops 16384 | bytes 98312 | tf_op jit(solution)/shard_map/sub | solution.py:126
  71.2 13.4 %all_gather.11 = f32[8,16,256]{2,1,0:T(8,128)S(1)} all-gather(f32[2,16,256]{2,1,0:T(8,128)S(1)} %pad_maximum_fusion.20), channel_id=1, replica_groups=mesh['gx'=4,'gy'=2,'gz'=4] {'gz'}, dimensions={0}, use_global_device_ids=true | all-gather | bytes 163840 | tf_op jit(solution)/shard_map/all_gather | solution.py:129
  84.9 0.8 select_select_fusion
  (82 shorter events, 2.0 us)
Async XLA Ops:
  1.0 8.5 %collective-permute-start = (f32[16,1,256]{2,1,0:T(1,128)S(1)}, f32[16,1,256]{2,1,0:T(1,128)S(1)}, u32[]{:S(2)}, u32[]{:S(2)}) collective-permute-start(f32[16,1,256]{2,1,0:T(1,128)S(1)} %get-tuple-element.94), channel_id=1, source_target_pairs={{8,0},{16,8},{24,16},{9,1},{17,9},{25,17},{10,2},{18,10},{26,18},{... | collective-permute-start | bytes 49160 | tf_op jit(solution)/shard_map/ppermute | solution.py:20
  4.3 6.5 %collective-permute-start.1 = (f32[16,1,256]{2,1,0:T(1,128)S(1)}, f32[16,1,256]{2,1,0:T(1,128)S(1)}, u32[]{:S(2)}, u32[]{:S(2)}) collective-permute-start(f32[16,1,256]{2,1,0:T(1,128)S(1)} %get-tuple-element.93), channel_id=1, source_target_pairs={{0,8},{8,16},{16,24},{1,9},{9,17},{17,25},{2,10},{10,18},{18,26},{... | collective-permute-start | bytes 49160 | tf_op jit(solution)/shard_map/ppermute | solution.py:17
  6.9 0.7 copy-start.4
  8.2 1.3 %copy-start.3 = (s32[16,256]{1,0:T(8,128)S(1)}, s32[16,256]{1,0:T(8,128)}, u32[]{:S(2)}) copy-start(s32[16,256]{1,0:T(8,128)} %param.9) | copy-start | bytes 49156
  8.2 2.7 %copy-start = (f32[16,16,256]{2,1,0:T(8,128)S(1)}, f32[16,16,256]{2,1,0:T(8,128)}, u32[]{:S(2)}) copy-start(f32[16,16,256]{2,1,0:T(8,128)} %param.5) | copy-start | bytes 786436
  10.9 5.7 %copy-start.1 = (f32[16,16,256]{2,1,0:T(8,128)S(1)}, f32[16,16,256]{2,1,0:T(8,128)}, u32[]{:S(2)}) copy-start(f32[16,16,256]{2,1,0:T(8,128)} %param.6) | copy-start | bytes 786436
  11.0 5.7 %copy-start.2 = (f32[16,16,256]{2,1,0:T(8,128)S(1)}, f32[16,16,256]{2,1,0:T(8,128)}, u32[]{:S(2)}) copy-start(f32[16,16,256]{2,1,0:T(8,128)} %param.7) | copy-start | bytes 786436
  11.1 4.6 %collective-permute-start.2 = (f32[16,18,1]{2,1,0:T(8,128)S(1)}, f32[16,18,1]{2,1,0:T(8,128)S(1)}, u32[]{:S(2)}, u32[]{:S(2)}) collective-permute-start(f32[16,18,1]{2,1,0:T(8,128)S(1)} %get-tuple-element.63), channel_id=1, source_target_pairs={{4,0},{5,1},{6,2},{7,3},{12,8},{13,9},{14,10},{15,11},{20,16},{21,... | collective-permute-start | bytes 3464 | tf_op jit(solution)/shard_map/ppermute | solution.py:20
  12.5 4.1 %collective-permute-start.3 = (f32[16,18,1]{2,1,0:T(8,128)S(1)}, f32[16,18,1]{2,1,0:T(8,128)S(1)}, u32[]{:S(2)}, u32[]{:S(2)}) collective-permute-start(f32[16,18,1]{2,1,0:T(8,128)S(1)} %get-tuple-element.64), channel_id=1, source_target_pairs={{0,4},{1,5},{2,6},{3,7},{8,12},{9,13},{10,14},{11,15},{16,20},{17,... | collective-permute-start | bytes 3464 | tf_op jit(solution)/shard_map/ppermute | solution.py:17
  53.8 5.9 %collective-permute-start.4 = (f32[16,1,256]{2,1,0:T(1,128)S(1)}, f32[16,1,256]{2,1,0:T(1,128)S(1)}, u32[]{:S(2)}, u32[]{:S(2)}) collective-permute-start(f32[16,1,256]{2,1,0:T(1,128)S(1)} %get-tuple-element.74), channel_id=1, source_target_pairs={{8,0},{16,8},{24,16},{9,1},{17,9},{25,17},{10,2},{18,10},{26,18},{... | collective-permute-start | bytes 49160 | tf_op jit(solution)/shard_map/ppermute | solution.py:20
  56.7 6.5 %collective-permute-start.5 = (f32[16,1,256]{2,1,0:T(1,128)S(1)}, f32[16,1,256]{2,1,0:T(1,128)S(1)}, u32[]{:S(2)}, u32[]{:S(2)}) collective-permute-start(f32[16,1,256]{2,1,0:T(1,128)S(1)} %get-tuple-element.73), channel_id=1, source_target_pairs={{0,8},{8,16},{16,24},{1,9},{9,17},{17,25},{2,10},{10,18},{18,26},{... | collective-permute-start | bytes 49160 | tf_op jit(solution)/shard_map/ppermute | solution.py:17
  63.4 4.4 %collective-permute-start.6 = (f32[16,18,1]{2,1,0:T(8,128)S(1)}, f32[16,18,1]{2,1,0:T(8,128)S(1)}, u32[]{:S(2)}, u32[]{:S(2)}) collective-permute-start(f32[16,18,1]{2,1,0:T(8,128)S(1)} %get-tuple-element.55), channel_id=1, source_target_pairs={{4,0},{5,1},{6,2},{7,3},{12,8},{13,9},{14,10},{15,11},{20,16},{21,... | collective-permute-start | bytes 3464 | tf_op jit(solution)/shard_map/ppermute | solution.py:20
  64.7 4.1 %collective-permute-start.7 = (f32[16,18,1]{2,1,0:T(8,128)S(1)}, f32[16,18,1]{2,1,0:T(8,128)S(1)}, u32[]{:S(2)}, u32[]{:S(2)}) collective-permute-start(f32[16,18,1]{2,1,0:T(8,128)S(1)} %get-tuple-element.56), channel_id=1, source_target_pairs={{0,4},{1,5},{2,6},{3,7},{8,12},{9,13},{10,14},{11,15},{16,20},{17,... | collective-permute-start | bytes 3464 | tf_op jit(solution)/shard_map/ppermute | solution.py:17
where the time goes:
time: 86.1 us; the launch traced here: 85.7 us
  blocking collectives  42.6 us (49%)
  starting transfers between devices  20.5 us (24%)
  other arithmetic  9.26 us (11%)
  waiting for transfers between devices  6.93 us (8%)
  local copies, waits for them, and re-layouts  5.68 us (7%)
    all_gather x2, blocking collectives, on_device(): all_sources = lax.all_gather(source_pair, 'gz', axis=0, tiled=True)  26.9 us
    all_gather x1, blocking collectives, on_device(): gathered = lax.all_gather(coupled, 'gz', axis=1, tiled=True)  15.6 us
    ppermute x4, starting transfers between devices, extended(): lax.ppermute(lax.slice_in_dim(block, block.shape[dim] - width, None, axis...  11.5 us
    ppermute x4, starting transfers between devices, extended(): lax.ppermute(lax.slice_in_dim(block, 0, width, axis=dim), axis, backward)  8.96 us
    ppermute x4, waiting for transfers between devices, extended(): lax.ppermute(lax.slice_in_dim(block, block.shape[dim] - width, None, axis...  6.92 us
    sub x2, other arithmetic, on_device(): first_source = source[0] - high_full[0] * interior[1]  2.43 us
    add x10, other arithmetic, apply_local(): source + weight_low * move_rows(source, stride, 0.0)  1.9 us
  transfers between devices with their start and end apart: 8, of which 4 were waited for; matrix products, arithmetic and copies ran while one was open for 2% of the time, Pallas kernels for 0%

commit v1 on v0

v1 whole, which is shorter than its diff:
```python
import functools

import jax
import jax.numpy as jnp
import numpy as np
from jax import lax
from jax.experimental import pallas as pl
from jax.experimental.pallas import tpu as pltpu
from jax.sharding import PartitionSpec as P

coef_z = 1000.0
coef_x = 0.3
coef_y = 0.2
bratu_lambda = 0.2
LANES = 128
MESH = pl.DeviceIdType.MESH


def relax_kernel(
    counts,
    level_ref,
    corr_hbm,
    res_hbm,
    state_hbm,
    colour_hbm,
    out_ref,
    corr,
    res,
    state,
    colour,
    iterate,
    inv,
    low_w,
    high_w,
    src,
    local,
    x_send,
    x_recv,
    y_recv,
    up_send,
    up_recv,
    down_send,
    down_recv,
    load_sem,
    x_send_sem,
    x_recv_sem,
    y_send_sem,
    y_recv_sem,
    up_send_sem,
    up_recv_sem,
    down_send_sem,
    down_recv_sem,
):
    nx, ny, nz = counts
    depth, wide_x, wide_y = corr.shape
    px, py, pz = (lax.axis_index(a) for a in ("gx", "gy", "gz"))
    total = depth * nz

    axes = (("gx", px, nx), ("gy", py, ny), ("gz", pz, nz))
    barrier = pltpu.get_barrier_semaphore()
    present = jnp.int32(0)
    for axis, place, count in axes:
        present = present + jnp.where(place > 0, 1, 0) + jnp.where(place < count - 1, 1, 0)

        @pl.when(place > 0)
        def _():
            pl.semaphore_signal(barrier, inc=1, device_id={axis: place - 1}, device_id_type=MESH)

        @pl.when(place < count - 1)
        def _():
            pl.semaphore_signal(barrier, inc=1, device_id={axis: place + 1}, device_id_type=MESH)

    loads = [
        pltpu.make_async_copy(a, b, load_sem.at[n])
        for n, (a, b) in enumerate(
            ((state_hbm, state), (corr_hbm, corr), (res_hbm, res), (colour_hbm, colour))
        )
    ]
    for load in loads:
        load.start()

    for side, gone in ((0, px == 0), (1, px == nx - 1)):

        @pl.when(gone)
        def _():
            for turn in range(2):
                x_recv[turn, side] = jnp.zeros((depth, wide_y), jnp.float32)

    for side, gone in ((0, py == 0), (1, py == ny - 1)):

        @pl.when(gone)
        def _():
            for turn in range(2):
                y_recv[turn, side] = jnp.zeros((depth, wide_x, LANES), jnp.float32)

    @pl.when(pz == 0)
    def _():
        up_recv[...] = jnp.zeros(up_recv.shape, jnp.float32)

    @pl.when(pz == nz - 1)
    def _():
        down_recv[...] = jnp.zeros(down_recv.shape, jnp.float32)

    def spread(tile):
        row = jnp.concatenate([tile] * (wide_y // LANES), 1)
        return jnp.concatenate([row] * (wide_x // 8), 0)

    powers = [np.float32(0.8) * np.float32(1.3**n) for n in range(4)]

    def spacing_at(index):
        level = level_ref[index]
        value = jnp.where(level == 0, powers[0], powers[1])
        value = jnp.where(level == 2, powers[2], value)
        return jnp.where(level == 3, powers[3], value)

    base = pz * depth
    spacing = [spacing_at(base + i) for i in range(depth)]
    before = spacing_at(jnp.maximum(base - 1, 0))
    after = spacing_at(jnp.minimum(base + depth, total - 1))
    chain = [before] + spacing + [after]
    faces = []
    for i in range(depth + 1):
        face = coef_z * 2.0 / jnp.full((8, LANES), chain[i] + chain[i + 1], jnp.float32)
        if i == 0:
            face = jnp.where(pz == 0, 0.0, face)
        if i == depth:
            face = jnp.where(pz == nz - 1, 0.0, face)
        faces.append(spread(face))
    face_first, face_last = faces[0], faces[depth]

    loads[0].wait()
    for i in range(depth):
        state[i] = (faces[i] + faces[i + 1]) + spacing[i] * (
            2.0 * coef_x + 2.0 * coef_y - bratu_lambda * jnp.exp(state[i])
        )
    forward = 1.0 / state[0]
    backward = 1.0 / state[depth - 1]
    inv[0] = forward
    low_w[depth - 1] = backward
    for i in range(1, depth):
        forward = 1.0 / (state[i] - faces[i] * faces[i] * forward)
        inv[i] = forward
        j = depth - 1 - i
        backward = 1.0 / (state[j] - faces[j + 1] * faces[j + 1] * backward)
        low_w[j] = backward
    high_w[depth - 1] = forward
    for i in range(1, depth):
        backward = backward * faces[i] * low_w[i]
        low_w[i] = backward
        j = depth - 1 - i
        forward = forward * faces[j + 1] * inv[j]
        high_w[j] = forward

    def x_copy(turn, side):
        return pltpu.make_async_remote_copy(
            src_ref=x_send.at[turn, side],
            dst_ref=x_recv.at[turn, 1 - side],
            send_sem=x_send_sem.at[turn, side],
            recv_sem=x_recv_sem.at[turn, 1 - side],
            device_id={"gx": px - 1 if side == 0 else px + 1},
            device_id_type=MESH,
        )

    def y_copy(turn, side):
        whole = corr if turn == 0 else iterate
        start = 0 if side == 0 else wide_y - LANES
        return pltpu.make_async_remote_copy(
            src_ref=whole.at[:, :, pl.ds(start, LANES)],
            dst_ref=y_recv.at[turn, 1 - side],
            send_sem=y_send_sem.at[turn, side],
            recv_sem=y_recv_sem.at[turn, 1 - side],
            device_id={"gy": py - 1 if side == 0 else py + 1},
            device_id_type=MESH,
        )

    def up_copy(slot):
        return pltpu.make_async_remote_copy(
            src_ref=up_send.at[slot],
            dst_ref=up_recv.at[slot],
            send_sem=up_send_sem.at[slot],
            recv_sem=up_recv_sem.at[slot],
            device_id={"gz": pz + 1},
            device_id_type=MESH,
        )

    def down_copy(slot):
        return pltpu.make_async_remote_copy(
            src_ref=down_send.at[slot],
            dst_ref=down_recv.at[slot],
            send_sem=down_send_sem.at[slot],
            recv_sem=down_recv_sem.at[slot],
            device_id={"gz": pz - 1},
            device_id_type=MESH,
        )

    def on_sides(place, count, action):
        for side, there in ((0, place > 0), (1, place < count - 1)):

            @pl.when(there)
            def _():
                action(side)

    def send_halos(turn):
        on_sides(px, nx, lambda side: x_copy(turn, side).start())
        on_sides(py, ny, lambda side: y_copy(turn, side).start())

    def wait_halos(turn):
        on_sides(py, ny, lambda side: y_copy(turn, 1 - side).wait_recv())
        on_sides(px, nx, lambda side: x_copy(turn, 1 - side).wait_recv())

    loads[1].wait()
    for i in range(depth):
        x_send[0, 0, pl.ds(i, 1)] = corr[i, pl.ds(0, 1)]
        x_send[0, 1, pl.ds(i, 1)] = corr[i, pl.ds(wide_x - 1, 1)]
    pl.semaphore_wait(barrier, present)
    send_halos(0)

    first_both = low_w[depth - 1]

    def up_factor():
        ratio = up_recv[0]
        gain = first_both * face_first / (1.0 - low_w[0] * face_first * ratio)
        return ratio, gain, face_last * (high_w[depth - 1] + first_both * gain * ratio)

    def down_factor():
        ratio = down_recv[0]
        gain = first_both * face_last / (1.0 - high_w[depth - 1] * face_last * ratio)
        return ratio, gain, face_first * (low_w[0] + first_both * gain * ratio)

    @pl.when((pz == 0) & (pz < nz - 1))
    def _():
        up_send[0] = up_factor()[2]
        up_copy(0).start()

    @pl.when((pz == nz - 1) & (pz > 0))
    def _():
        down_send[0] = down_factor()[2]
        down_copy(0).start()

    loads[2].wait()
    loads[3].wait()

    rows = lax.broadcasted_iota(jnp.int32, (wide_x, wide_y), 0)
    columns = lax.broadcasted_iota(jnp.int32, (wide_x, wide_y), 1)
    narrow = lax.broadcasted_iota(jnp.int32, (wide_x, LANES), 1)
    x_first, x_last = rows == 0, rows == wide_x - 1
    y_first, y_last = columns == 0, columns == wide_y - 1

    for turn in range(2):
        held = corr if turn == 0 else iterate
        for i in range(depth):
            plane = held[i]
            beside = coef_x * (
                jnp.where(x_first, 0.0, pltpu.roll(plane, 1, 0))
                + jnp.where(x_last, 0.0, pltpu.roll(plane, wide_x - 1, 0))
            ) + coef_y * (
                jnp.where(y_first, 0.0, pltpu.roll(plane, 1, 1))
                + jnp.where(y_last, 0.0, pltpu.roll(plane, wide_y - 1, 1))
            )
            src[i] = spacing[i] * (res[i] + beside)
        wait_halos(turn)
        first_value = jnp.zeros((wide_x, wide_y), jnp.float32)
        last_value = first_value
        for i in range(depth):
            halo_x = jnp.where(
                x_first,
                x_recv[turn, 0, pl.ds(i, 1)],
                jnp.where(x_last, x_recv[turn, 1, pl.ds(i, 1)], 0.0),
            )
            halo_low = jnp.where(narrow == 0, pltpu.roll(y_recv[turn, 0, i], 1, 1), 0.0)
            halo_high = jnp.where(
                narrow == LANES - 1, pltpu.roll(y_recv[turn, 1, i], LANES - 1, 1), 0.0
            )
            if wide_y == LANES:
                halo_y = halo_low + halo_high
            else:
                middle = [jnp.zeros((wide_x, LANES), jnp.float32)] * (wide_y // LANES - 2)
                halo_y = jnp.concatenate([halo_low] + middle + [halo_high], 1)
            source = src[i] + spacing[i] * (coef_x * halo_x + coef_y * halo_y)
            src[i] = source
            first_value = first_value + low_w[i] * source
            last_value = last_value + high_w[i] * source

        slot = 1 + turn

        def up_value():
            ratio, gain, _ = up_factor()
            return gain * (up_recv[slot] + ratio * first_value) + last_value

        def down_value():
            ratio, gain, _ = down_factor()
            return gain * (down_recv[slot] + ratio * last_value) + first_value

        @pl.when((pz == 0) & (pz < nz - 1))
        def _():
            up_send[slot] = last_value
            up_copy(slot).start()

        @pl.when((pz == nz - 1) & (pz > 0))
        def _():
            down_send[slot] = first_value
            down_copy(slot).start()

        value = src[0] * inv[0]
        src[0] = value
        for i in range(1, depth):
            value = (src[i] + faces[i] * value) * inv[i]
            src[i] = value
        local[depth - 1] = value
        for i in range(depth - 2, -1, -1):
            value = src[i] + faces[i + 1] * inv[i] * value
            local[i] = value

        def pass_up():
            @pl.when(pz > 0)
            def _():
                if turn == 0:
                    up_copy(0).wait_recv()

                    @pl.when(pz < nz - 1)
                    def _():
                        up_send[0] = up_factor()[2]
                        up_copy(0).start()

                up_copy(slot).wait_recv()

                @pl.when(pz < nz - 1)
                def _():
                    up_send[slot] = up_value()
                    up_copy(slot).start()

        def pass_down():
            @pl.when(pz < nz - 1)
            def _():
                if turn == 0:
                    down_copy(0).wait_recv()

                    @pl.when(pz > 0)
                    def _():
                        down_send[0] = down_factor()[2]
                        down_copy(0).start()

                down_copy(slot).wait_recv()

                @pl.when(pz > 0)
                def _():
                    down_send[slot] = down_value()
                    down_copy(slot).start()

        upper_half = 2 * pz > nz - 1

        @pl.when(upper_half)
        def _():
            pass_down()

        pass_up()

        @pl.when(jnp.logical_not(upper_half))
        def _():
            pass_down()

        up_ratio, up_gain, up_next = up_factor()
        down_ratio = down_recv[0]
        below, above = up_recv[slot], down_recv[slot]
        carried = up_gain * (below + up_ratio * first_value) + last_value
        last_cell = (carried + up_next * above) / (1.0 - up_next * down_ratio)
        from_above = face_last * (down_ratio * last_cell + above)
        first_cell = (
            low_w[0] * face_first * below + first_both * from_above + first_value
        ) / (1.0 - low_w[0] * face_first * up_ratio)
        from_below = face_first * (up_ratio * first_cell + below)
        chosen = colour[...] == turn
        for i in range(depth):
            solved = local[i] + low_w[i] * from_below + high_w[i] * from_above
            fresh = jnp.where(chosen, solved, held[i])
            if turn == 0:
                iterate[i] = fresh
                x_send[1, 0, pl.ds(i, 1)] = fresh[0:1]
                x_send[1, 1, pl.ds(i, 1)] = fresh[wide_x - 1 : wide_x]
            else:
                out_ref[i] = fresh
        if turn == 0:
            send_halos(1)

    for turn in range(2):
        on_sides(px, nx, lambda side: x_copy(turn, side).wait_send())
        on_sides(py, ny, lambda side: y_copy(turn, side).wait_send())
    for slot in range(3):

        @pl.when(pz < nz - 1)
        def _():
            up_copy(slot).wait_send()

        @pl.when(pz > 0)
        def _():
            down_copy(slot).wait_send()


def on_device(counts, correction, residual, state, spacing_level, line_colour):
    block = correction.shape
    depth, wide_x, wide_y = block
    plane = (wide_x, wide_y)
    f32 = jnp.float32
    dma = pltpu.SemaphoreType.DMA
    anywhere = pl.BlockSpec(memory_space=pl.ANY)
    return pl.pallas_call(
        functools.partial(relax_kernel, counts),
        out_shape=jax.ShapeDtypeStruct(block, f32),
        in_specs=[pl.BlockSpec(memory_space=pltpu.SMEM)] + [anywhere] * 4,
        out_specs=pl.BlockSpec(memory_space=pltpu.VMEM),
        scratch_shapes=[
            pltpu.VMEM(block, f32),
            pltpu.VMEM(block, f32),
            pltpu.VMEM(block, f32),
            pltpu.VMEM(plane, jnp.int32),
            pltpu.VMEM(block, f32),
            pltpu.VMEM(block, f32),
            pltpu.VMEM(block, f32),
            pltpu.VMEM(block, f32),
            pltpu.VMEM(block, f32),
            pltpu.VMEM(block, f32),
            pltpu.VMEM((2, 2, depth, wide_y), f32),
            pltpu.VMEM((2, 2, depth, wide_y), f32),
            pltpu.VMEM((2, 2, depth, wide_x, LANES), f32),
            pltpu.VMEM((3,) + plane, f32),
            pltpu.VMEM((3,) + plane, f32),
            pltpu.VMEM((3,) + plane, f32),
            pltpu.VMEM((3,) + plane, f32),
            dma((4,)),
            dma((2, 2)),
            dma((2, 2)),
            dma((2, 2)),
            dma((2, 2)),
            dma((3,)),
            dma((3,)),
            dma((3,)),
            dma((3,)),
        ],
        compiler_params=pltpu.CompilerParams(collective_id=0, has_side_effects=True),
    )(spacing_level, correction, residual, state, line_colour)


def solution(mesh):
    counts = tuple(mesh.shape[a] for a in ("gx", "gy", "gz"))
    return jax.shard_map(
        functools.partial(on_device, counts),
        mesh=mesh,
        in_specs=(
            P("gz", "gx", "gy"),
            P("gz", "gx", "gy"),
            P("gz", "gx", "gy"),
            P(),
            P("gx", "gy"),
        ),
        out_specs=P("gz", "gx", "gy"),
        check_vma=False,
    )
```

time: 86.1 us -> 29.9 us (0.35)
  the two profiles are of different devices: /device:TPU:12 before, /device:TPU:0 now
where the time goes in v1:
time: 29.9 us; the launch traced here: 29.8 us
  Pallas kernels  28.1 us (94%)
  local copies, waits for them, and re-layouts  1.67 us (6%)
    pallas_call x1, Pallas kernels, on_device(): pl.pallas_call(functools.partial(relax_kernel, counts), out_shape=jax.Sha...  28.1 us
    unnamed x1, local copies, waits for them, and re-layouts  1.67 us

profile of v1, /device:TPU:0, one launch (start us, length us, event | category | flops | bytes accessed | tf_op | source)
XLA Modules:
  0.0 29.8 jit_solution(7138205735000618926)
XLA Ops:
  0.0 28.1 %shard_map.55 = f32[16,16,256]{2,1,0:T(8,128)} custom-call(s32[64]{0:T(128)} %level_ref.1, f32[16,16,256]{2,1,0:T(8,128)} %corr_hbm.1, f32[16,16,256]{2,1,0:T(8,128)} %res_hbm.1, f32[16,16,256]{2,1,0:T(8,128)} %state_hbm.1, s32[16,256]{1,0:T(8,128)} %colour_hbm.1), custom_call_target="tpu_custom_call" | custom-call | tf_op jit(solution)/shard_map/pallas_call | solution.py:406
  28.1 1.7 %copy.7 = f32[16,16,256]{2,1,0:T(8,128)} copy(f32[16,16,256]{2,1,0:T(8,128)} %shard_map.55) | data formatting | bytes 524288

commit v2 on v1

--- a/solution.py
+++ b/solution.py
@@ -37,26 +37,27 @@
     x_send,
     x_recv,
     y_recv,
-    up_send,
-    up_recv,
-    down_send,
-    down_recv,
+    factor_send,
+    factor_recv,
+    gains,
+    sum_send,
+    sum_recv,
     load_sem,
     x_send_sem,
     x_recv_sem,
     y_send_sem,
     y_recv_sem,
-    up_send_sem,
-    up_recv_sem,
-    down_send_sem,
-    down_recv_sem,
+    factor_send_sem,
+    factor_recv_sem,
+    sum_send_sem,
+    sum_recv_sem,
 ):
     nx, ny, nz = counts
     depth, wide_x, wide_y = corr.shape
     px, py, pz = (lax.axis_index(a) for a in ("gx", "gy", "gz"))
     total = depth * nz
 
-    axes = (("gx", px, nx), ("gy", py, ny), ("gz", pz, nz))
+    axes = (("gx", px, nx), ("gy", py, ny))
     barrier = pltpu.get_barrier_semaphore()
     present = jnp.int32(0)
     for axis, place, count in axes:
@@ -70,6 +71,17 @@
         def _():
             pl.semaphore_signal(barrier, inc=1, device_id={axis: place + 1}, device_id_type=MESH)
 
+    for step in range(1, nz):
+        present = present + jnp.where(pz >= step, 1, 0) + jnp.where(pz + step < nz, 1, 0)
+
+        @pl.when(pz >= step)
+        def _():
+            pl.semaphore_signal(barrier, inc=1, device_id={"gz": pz - step}, device_id_type=MESH)
+
+        @pl.when(pz + step < nz)
+        def _():
+            pl.semaphore_signal(barrier, inc=1, device_id={"gz": pz + step}, device_id_type=MESH)
+
     loads = [
         pltpu.make_async_copy(a, b, load_sem.at[n])
         for n, (a, b) in enumerate(
@@ -93,13 +105,20 @@
             for turn in range(2):
                 y_recv[turn, side] = jnp.zeros((depth, wide_x, LANES), jnp.float32)
 
-    @pl.when(pz == 0)
-    def _():
-        up_recv[...] = jnp.zeros(up_recv.shape, jnp.float32)
-
-    @pl.when(pz == nz - 1)
-    def _():
-        down_recv[...] = jnp.zeros(down_recv.shape, jnp.float32)
+    ends = (pz == 0, pz == nz - 1)
+    below_count = (pz, nz - 1 - pz)
+    for way in range(2):
+
+        @pl.when(ends[way])
+        def _():
+            factor_recv[way] = jnp.zeros(factor_recv.shape[1:], jnp.float32)
+
+        for step in range(1, nz):
+
+            @pl.when(below_count[way] < step)
+            def _():
+                for turn in range(2):
+                    sum_recv[turn, way, step - 1] = jnp.zeros((wide_x, wide_y), jnp.float32)
 
     def spread(tile):
         row = jnp.concatenate([tile] * (wide_y // LANES), 1)
@@ -173,23 +192,23 @@
             device_id_type=MESH,
         )
 
-    def up_copy(slot):
+    def factor_copy(way):
         return pltpu.make_async_remote_copy(
-            src_ref=up_send.at[slot],
-            dst_ref=up_recv.at[slot],
-            send_sem=up_send_sem.at[slot],
-            recv_sem=up_recv_sem.at[slot],
-            device_id={"gz": pz + 1},
+            src_ref=factor_send.at[way],
+            dst_ref=factor_recv.at[way],
+            send_sem=factor_send_sem.at[way],
+            recv_sem=factor_recv_sem.at[way],
+            device_id={"gz": pz + 1 - 2 * way},
             device_id_type=MESH,
         )
 
-    def down_copy(slot):
+    def sum_copy(turn, way, step):
         return pltpu.make_async_remote_copy(
-            src_ref=down_send.at[slot],
-            dst_ref=down_recv.at[slot],
-            send_sem=down_send_sem.at[slot],
-            recv_sem=down_recv_sem.at[slot],
-            device_id={"gz": pz - 1},
+            src_ref=sum_send.at[turn, way],
+            dst_ref=sum_recv.at[turn, way, step - 1],
+            send_sem=sum_send_sem.at[turn, way, step - 1],
+            recv_sem=sum_recv_sem.at[turn, way, step - 1],
+            device_id={"gz": pz + step * (1 - 2 * way)},
             device_id_type=MESH,
         )
 
@@ -217,25 +236,30 @@
 
     first_both = low_w[depth - 1]
 
-    def up_factor():
-        ratio = up_recv[0]
-        gain = first_both * face_first / (1.0 - low_w[0] * face_first * ratio)
-        return ratio, gain, face_last * (high_w[depth - 1] + first_both * gain * ratio)
-
-    def down_factor():
-        ratio = down_recv[0]
-        gain = first_both * face_last / (1.0 - high_w[depth - 1] * face_last * ratio)
-        return ratio, gain, face_first * (low_w[0] + first_both * gain * ratio)
-
-    @pl.when((pz == 0) & (pz < nz - 1))
-    def _():
-        up_send[0] = up_factor()[2]
-        up_copy(0).start()
-
-    @pl.when((pz == nz - 1) & (pz > 0))
-    def _():
-        down_send[0] = down_factor()[2]
-        down_copy(0).start()
+    own = (low_w.at[0], high_w.at[depth - 1])
+    near_face, far_face = (face_first, face_last), (face_last, face_first)
+
+    def pass_factor(way):
+        ratio, scale = factor_recv[way, 0], factor_recv[way, 1]
+        gain = first_both * near_face[way] / (1.0 - own[way][...] * near_face[way] * ratio)
+        ahead = far_face[way] * (own[1 - way][...] + first_both * gain * ratio)
+        scale = jnp.where(ends[way], 1.0, gain * scale)
+        gains[way, 0] = gain
+        gains[way, 1] = gain * ratio
+        gains[way, 2] = ahead
+        gains[way, 3] = 1.0 / scale
+
+        @pl.when(jnp.logical_not(ends[1 - way]))
+        def _():
+            factor_send[way, 0] = ahead
+            factor_send[way, 1] = scale
+            factor_copy(way).start()
+
+    for way in range(2):
+
+        @pl.when(ends[way])
+        def _():
+            pass_factor(way)
 
     loads[2].wait()
     loads[3].wait()
@@ -281,25 +305,44 @@
             first_value = first_value + low_w[i] * source
             last_value = last_value + high_w[i] * source
 
-        slot = 1 + turn
-
-        def up_value():
-            ratio, gain, _ = up_factor()
-            return gain * (up_recv[slot] + ratio * first_value) + last_value
-
-        def down_value():
-            ratio, gain, _ = down_factor()
-            return gain * (down_recv[slot] + ratio * last_value) + first_value
-
-        @pl.when((pz == 0) & (pz < nz - 1))
-        def _():
-            up_send[slot] = last_value
-            up_copy(slot).start()
-
-        @pl.when((pz == nz - 1) & (pz > 0))
-        def _():
-            down_send[slot] = first_value
-            down_copy(slot).start()
+        edge_values = (first_value, last_value)
+
+        def send_sums(way):
+            @pl.when(jnp.logical_not(ends[1 - way]))
+            def _():
+                sum_send[turn, way] = gains[way, 3] * (
+                    gains[way, 1] * edge_values[way] + edge_values[1 - way]
+                )
+                for step in range(nz - 1, 0, -1):
+
+                    @pl.when(below_count[1 - way] >= step)
+                    def _():
+                        sum_copy(turn, way, step).start()
+
+        def advance(way):
+            @pl.when(jnp.logical_not(ends[way]))
+            def _():
+                factor_copy(way).wait_recv()
+                pass_factor(way)
+
+            send_sums(way)
+
+        if turn == 0:
+            upper_half = 2 * pz > nz - 1
+
+            @pl.when(upper_half)
+            def _():
+                advance(1)
+
+            advance(0)
+
+            @pl.when(jnp.logical_not(upper_half))
+            def _():
+                advance(1)
+
+        else:
+            send_sums(0)
+            send_sums(1)
 
         value = src[0] * inv[0]
         src[0] = value
@@ -311,58 +354,23 @@
             value = src[i] + faces[i + 1] * inv[i] * value
             local[i] = value
 
-        def pass_up():
-            @pl.when(pz > 0)
-            def _():
-                if turn == 0:
-                    up_copy(0).wait_recv()
-
-                    @pl.when(pz < nz - 1)
-                    def _():
-                        up_send[0] = up_factor()[2]
-                        up_copy(0).start()
-
-                up_copy(slot).wait_recv()
-
-                @pl.when(pz < nz - 1)
+        arrived = []
+        for way in range(2):
+            for step in range(1, nz):
+
+                @pl.when(below_count[way] >= step)
                 def _():
-                    up_send[slot] = up_value()
-                    up_copy(slot).start()
-
-        def pass_down():
-            @pl.when(pz < nz - 1)
-            def _():
-                if turn == 0:
-                    down_copy(0).wait_recv()
-
-                    @pl.when(pz > 0)
-                    def _():
-                        down_send[0] = down_factor()[2]
-                        down_copy(0).start()
-
-                down_copy(slot).wait_recv()
-
-                @pl.when(pz > 0)
-                def _():
-                    down_send[slot] = down_value()
-                    down_copy(slot).start()
-
-        upper_half = 2 * pz > nz - 1
-
-        @pl.when(upper_half)
-        def _():
-            pass_down()
-
-        pass_up()
-
-        @pl.when(jnp.logical_not(upper_half))
-        def _():
-            pass_down()
-
-        up_ratio, up_gain, up_next = up_factor()
-        down_ratio = down_recv[0]
-        below, above = up_recv[slot], down_recv[slot]
-        carried = up_gain * (below + up_ratio * first_value) + last_value
+                    sum_copy(turn, way, step).wait_recv()
+
+        for way in range(2):
+            value = sum_recv[turn, way, 0]
+            for step in range(2, nz):
+                value = value + sum_recv[turn, way, step - 1]
+            arrived.append(factor_recv[way, 1] * value)
+        below, above = arrived
+        up_ratio, down_ratio = factor_recv[0, 0], factor_recv[1, 0]
+        up_next = gains[0, 2]
+        carried = gains[0, 0] * below + gains[0, 1] * first_value + last_value
         last_cell = (carried + up_next * above) / (1.0 - up_next * down_ratio)
         from_above = face_last * (down_ratio * last_cell + above)
         first_cell = (
@@ -385,15 +393,18 @@
     for turn in range(2):
         on_sides(px, nx, lambda side: x_copy(turn, side).wait_send())
         on_sides(py, ny, lambda side: y_copy(turn, side).wait_send())
-    for slot in range(3):
-
-        @pl.when(pz < nz - 1)
-        def _():
-            up_copy(slot).wait_send()
-
-        @pl.when(pz > 0)
-        def _():
-            down_copy(slot).wait_send()
+    for way in range(2):
+
+        @pl.when(jnp.logical_not(ends[1 - way]))
+        def _():
+            factor_copy(way).wait_send()
+
+        for step in range(1, nz):
+
+            @pl.when(below_count[1 - way] >= step)
+            def _():
+                for turn in range(2):
+                    sum_copy(turn, way, step).wait_send()
 
 
 def on_device(counts, correction, residual, state, spacing_level, line_colour):
@@ -402,6 +413,7 @@
     plane = (wide_x, wide_y)
     f32 = jnp.float32
     dma = pltpu.SemaphoreType.DMA
+    others = max(counts[2] - 1, 1)
     anywhere = pl.BlockSpec(memory_space=pl.ANY)
     return pl.pallas_call(
         functools.partial(relax_kernel, counts),
@@ -422,19 +434,20 @@
             pltpu.VMEM((2, 2, depth, wide_y), f32),
             pltpu.VMEM((2, 2, depth, wide_y), f32),
             pltpu.VMEM((2, 2, depth, wide_x, LANES), f32),
-            pltpu.VMEM((3,) + plane, f32),
-            pltpu.VMEM((3,) + plane, f32),
-            pltpu.VMEM((3,) + plane, f32),
-            pltpu.VMEM((3,) + plane, f32),
+            pltpu.VMEM((2, 2) + plane, f32),
+            pltpu.VMEM((2, 2) + plane, f32),
+            pltpu.VMEM((2, 4) + plane, f32),
+            pltpu.VMEM((2, 2) + plane, f32),
+            pltpu.VMEM((2, 2, others) + plane, f32),
             dma((4,)),
             dma((2, 2)),
             dma((2, 2)),
             dma((2, 2)),
             dma((2, 2)),
-            dma((3,)),
-            dma((3,)),
-            dma((3,)),
-            dma((3,)),
+            dma((2,)),
+            dma((2,)),
+            dma((2, 2, others)),
+            dma((2, 2, others)),
         ],
         compiler_params=pltpu.CompilerParams(collective_id=0, has_side_effects=True),
     )(spacing_level, correction, residual, state, line_colour)

time: 29.9 us -> 24.9 us (0.83)
  Pallas kernels: 28.1 us -> 23.1 us
    pallas_call x1, Pallas kernels: 28.1 us -> 23.1 us  [on_device(): pl.pallas_call(functools.partial(relax_kernel, counts), out_shape=jax.Sha...]
where the time goes in v2:
time: 24.9 us; the launch traced here: 24.8 us
  Pallas kernels  23.1 us (93%)
  local copies, waits for them, and re-layouts  1.67 us (7%)
    pallas_call x1, Pallas kernels, on_device(): pl.pallas_call(functools.partial(relax_kernel, counts), out_shape=jax.Sha...  23.1 us
    unnamed x1, local copies, waits for them, and re-layouts  1.67 us

profile of v2, /device:TPU:0, one launch (start us, length us, event | category | flops | bytes accessed | tf_op | source)
XLA Modules:
  0.0 24.8 jit_solution(17296363947066428588)
XLA Ops:
  0.0 23.1 %shard_map.55 = f32[16,16,256]{2,1,0:T(8,128)} custom-call(s32[64]{0:T(128)} %level_ref.1, f32[16,16,256]{2,1,0:T(8,128)} %corr_hbm.1, f32[16,16,256]{2,1,0:T(8,128)} %res_hbm.1, f32[16,16,256]{2,1,0:T(8,128)} %state_hbm.1, s32[16,256]{1,0:T(8,128)} %colour_hbm.1), custom_call_target="tpu_custom_call" | custom-call | tf_op jit(solution)/shard_map/pallas_call | solution.py:418
  23.1 1.7 %copy.7 = f32[16,16,256]{2,1,0:T(8,128)} copy(f32[16,16,256]{2,1,0:T(8,128)} %shard_map.55) | data formatting | bytes 524288

commit v3 on v2

--- a/solution.py
+++ b/solution.py
@@ -29,9 +29,10 @@
     state,
     colour,
     iterate,
-    inv,
     low_w,
-    high_w,
+    grow,
+    grow_scale,
+    high_last,
     src,
     local,
     x_send,
@@ -137,38 +138,48 @@
     before = spacing_at(jnp.maximum(base - 1, 0))
     after = spacing_at(jnp.minimum(base + depth, total - 1))
     chain = [before] + spacing + [after]
-    faces = []
+    faces, widths = [], []
     for i in range(depth + 1):
-        face = coef_z * 2.0 / jnp.full((8, LANES), chain[i] + chain[i + 1], jnp.float32)
+        width = jnp.full((8, LANES), chain[i] + chain[i + 1], jnp.float32)
+        face = coef_z * 2.0 / width
         if i == 0:
             face = jnp.where(pz == 0, 0.0, face)
         if i == depth:
             face = jnp.where(pz == nz - 1, 0.0, face)
         faces.append(spread(face))
+        widths.append(spread(width * (0.5 / coef_z)))
     face_first, face_last = faces[0], faces[depth]
 
+    loads[1].wait()
+    for i in range(depth):
+        x_send[0, 0, pl.ds(i, 1)] = corr[i, pl.ds(0, 1)]
+        x_send[0, 1, pl.ds(i, 1)] = corr[i, pl.ds(wide_x - 1, 1)]
     loads[0].wait()
     for i in range(depth):
         state[i] = (faces[i] + faces[i + 1]) + spacing[i] * (
             2.0 * coef_x + 2.0 * coef_y - bratu_lambda * jnp.exp(state[i])
         )
-    forward = 1.0 / state[0]
-    backward = 1.0 / state[depth - 1]
-    inv[0] = forward
-    low_w[depth - 1] = backward
-    for i in range(1, depth):
-        forward = 1.0 / (state[i] - faces[i] * faces[i] * forward)
-        inv[i] = forward
+    fore_last, fore = jnp.zeros((wide_x, wide_y), jnp.float32), None
+    back_last, back = fore_last, None
+    for i in range(depth):
         j = depth - 1 - i
-        backward = 1.0 / (state[j] - faces[j + 1] * faces[j + 1] * backward)
-        low_w[j] = backward
-    high_w[depth - 1] = forward
-    for i in range(1, depth):
-        backward = backward * faces[i] * low_w[i]
-        low_w[i] = backward
-        j = depth - 1 - i
-        forward = forward * faces[j + 1] * inv[j]
-        high_w[j] = forward
+        if i == 0:
+            fore = back = jnp.ones((wide_x, wide_y), jnp.float32)
+        else:
+            fore_last, fore = fore, fore_next * widths[i]
+            back_last, back = back, back_next * widths[j + 1]
+        grow[i] = fore
+        low_w[j] = back
+        fore_next = state[i] * fore
+        back_next = state[j] * back
+        if i > 0:
+            fore_next = fore_next - faces[i] * fore_last
+            back_next = back_next - faces[j + 1] * back_last
+    grow_scale[...] = 1.0 / fore_next
+    back_scale = 1.0 / back_next
+    for i in range(depth):
+        low_w[i] = low_w[i] * back_scale
+    high_last[...] = grow[depth - 1] * grow_scale[...]
 
     def x_copy(turn, side):
         return pltpu.make_async_remote_copy(
@@ -192,12 +203,12 @@
             device_id_type=MESH,
         )
 
-    def factor_copy(way):
+    def factor_copy(way, part):
         return pltpu.make_async_remote_copy(
-            src_ref=factor_send.at[way],
-            dst_ref=factor_recv.at[way],
-            send_sem=factor_send_sem.at[way],
-            recv_sem=factor_recv_sem.at[way],
+            src_ref=factor_send.at[way, part],
+            dst_ref=factor_recv.at[way, part],
+            send_sem=factor_send_sem.at[way, part],
+            recv_sem=factor_recv_sem.at[way, part],
             device_id={"gz": pz + 1 - 2 * way},
             device_id_type=MESH,
         )
@@ -227,39 +238,44 @@
         on_sides(py, ny, lambda side: y_copy(turn, 1 - side).wait_recv())
         on_sides(px, nx, lambda side: x_copy(turn, 1 - side).wait_recv())
 
-    loads[1].wait()
-    for i in range(depth):
-        x_send[0, 0, pl.ds(i, 1)] = corr[i, pl.ds(0, 1)]
-        x_send[0, 1, pl.ds(i, 1)] = corr[i, pl.ds(wide_x - 1, 1)]
     pl.semaphore_wait(barrier, present)
     send_halos(0)
 
     first_both = low_w[depth - 1]
 
-    own = (low_w.at[0], high_w.at[depth - 1])
+    own = (low_w.at[0], high_last)
     near_face, far_face = (face_first, face_last), (face_last, face_first)
 
     def pass_factor(way):
-        ratio, scale = factor_recv[way, 0], factor_recv[way, 1]
+        ratio = factor_recv[way, 0]
         gain = first_both * near_face[way] / (1.0 - own[way][...] * near_face[way] * ratio)
         ahead = far_face[way] * (own[1 - way][...] + first_both * gain * ratio)
-        scale = jnp.where(ends[way], 1.0, gain * scale)
+
+        @pl.when(jnp.logical_not(ends[1 - way]))
+        def _():
+            factor_send[way, 0] = ahead
+            factor_copy(way, 0).start()
+
         gains[way, 0] = gain
         gains[way, 1] = gain * ratio
         gains[way, 2] = ahead
+
+    def pass_scale(way):
+        scale = jnp.where(ends[way], 1.0, gains[way, 0] * factor_recv[way, 1])
+
+        @pl.when(jnp.logical_not(ends[1 - way]))
+        def _():
+            factor_send[way, 1] = scale
+            factor_copy(way, 1).start()
+
         gains[way, 3] = 1.0 / scale
 
-        @pl.when(jnp.logical_not(ends[1 - way]))
-        def _():
-            factor_send[way, 0] = ahead
-            factor_send[way, 1] = scale
-            factor_copy(way).start()
-
     for way in range(2):
 
         @pl.when(ends[way])
         def _():
             pass_factor(way)
+            pass_scale(way)
 
     loads[2].wait()
     loads[3].wait()
@@ -284,7 +300,7 @@
             src[i] = spacing[i] * (res[i] + beside)
         wait_halos(turn)
         first_value = jnp.zeros((wide_x, wide_y), jnp.float32)
-        last_value = first_value
+        last_sum = first_value
         for i in range(depth):
             halo_x = jnp.where(
                 x_first,
@@ -303,8 +319,10 @@
             source = src[i] + spacing[i] * (coef_x * halo_x + coef_y * halo_y)
             src[i] = source
             first_value = first_value + low_w[i] * source
-            last_value = last_value + high_w[i] * source
-
+            local[i] = last_sum
+            last_sum = last_sum + grow[i] * source
+
+        last_value = last_sum * grow_scale[...]
         edge_values = (first_value, last_value)
 
         def send_sums(way):
@@ -322,8 +340,10 @@
         def advance(way):
             @pl.when(jnp.logical_not(ends[way]))
             def _():
-                factor_copy(way).wait_recv()
+                factor_copy(way, 0).wait_recv()
                 pass_factor(way)
+                factor_copy(way, 1).wait_recv()
+                pass_scale(way)
 
             send_sums(way)
 
@@ -343,16 +363,6 @@
         else:
             send_sums(0)
             send_sums(1)
-
-        value = src[0] * inv[0]
-        src[0] = value
-        for i in range(1, depth):
-            value = (src[i] + faces[i] * value) * inv[i]
-            src[i] = value
-        local[depth - 1] = value
-        for i in range(depth - 2, -1, -1):
-            value = src[i] + faces[i + 1] * inv[i] * value
-            local[i] = value
 
         arrived = []
         for way in range(2):
@@ -378,8 +388,10 @@
         ) / (1.0 - low_w[0] * face_first * up_ratio)
         from_below = face_first * (up_ratio * first_cell + below)
         chosen = colour[...] == turn
-        for i in range(depth):
-            solved = local[i] + low_w[i] * from_below + high_w[i] * from_above
+        ahead_sum = from_above * grow_scale[...]
+        for i in range(depth - 1, -1, -1):
+            ahead_sum = ahead_sum + low_w[i] * src[i]
+            solved = grow[i] * ahead_sum + low_w[i] * (local[i] + from_below)
             fresh = jnp.where(chosen, solved, held[i])
             if turn == 0:
                 iterate[i] = fresh
@@ -397,7 +409,8 @@
 
         @pl.when(jnp.logical_not(ends[1 - way]))
         def _():
-            factor_copy(way).wait_send()
+            factor_copy(way, 0).wait_send()
+            factor_copy(way, 1).wait_send()
 
         for step in range(1, nz):
 
@@ -417,7 +430,7 @@
     anywhere = pl.BlockSpec(memory_space=pl.ANY)
     return pl.pallas_call(
         functools.partial(relax_kernel, counts),
-        out_shape=jax.ShapeDtypeStruct(block, f32),
+        out_shape=pltpu.VMEM(block, f32),
         in_specs=[pl.BlockSpec(memory_space=pltpu.SMEM)] + [anywhere] * 4,
         out_specs=pl.BlockSpec(memory_space=pltpu.VMEM),
         scratch_shapes=[
@@ -428,7 +441,8 @@
             pltpu.VMEM(block, f32),
             pltpu.VMEM(block, f32),
             pltpu.VMEM(block, f32),
-            pltpu.VMEM(block, f32),
+            pltpu.VMEM(plane, f32),
+            pltpu.VMEM(plane, f32),
             pltpu.VMEM(block, f32),
             pltpu.VMEM(block, f32),
             pltpu.VMEM((2, 2, depth, wide_y), f32),
@@ -444,8 +458,8 @@
             dma((2, 2)),
             dma((2, 2)),
             dma((2, 2)),
-            dma((2,)),
-            dma((2,)),
+            dma((2, 2)),
+            dma((2, 2)),
             dma((2, 2, others)),
             dma((2, 2, others)),
         ],

time: 24.9 us -> 23.1 us (0.928)
  local copies, waits for them, and re-layouts: 1.67 us -> 0.71 us
  Pallas kernels: 23.1 us -> 22.2 us
    unnamed x1, local copies, waits for them, and re-layouts: 1.67 us -> 0.71 us
    pallas_call x1, Pallas kernels: 23.1 us -> 22.2 us  [on_device(): pl.pallas_call(functools.partial(relax_kernel, counts), out_shape=pltpu.V...]
where the time goes in v3:
time: 23.1 us; the launch traced here: 23 us
  Pallas kernels  22.2 us (96%)
  local copies, waits for them, and re-layouts  0.71 us (3%)
    pallas_call x1, Pallas kernels, on_device(): pl.pallas_call(functools.partial(relax_kernel, counts), out_shape=pltpu.V...  22.2 us
    unnamed x1, local copies, waits for them, and re-layouts  0.71 us

profile of v3, /device:TPU:0, one launch (start us, length us, event | category | flops | bytes accessed | tf_op | source)
XLA Modules:
  0.0 23.0 jit_solution(12187980463535504802)
XLA Ops:
  0.0 22.2 %shard_map.55 = f32[16,16,256]{2,1,0:T(8,128)S(1)} custom-call(s32[64]{0:T(128)} %level_ref.1, f32[16,16,256]{2,1,0:T(8,128)} %corr_hbm.1, f32[16,16,256]{2,1,0:T(8,128)} %res_hbm.1, f32[16,16,256]{2,1,0:T(8,128)} %state_hbm.1, s32[16,256]{1,0:T(8,128)} %colour_hbm.1), custom_call_target="tpu_custom_call" | custom-call | tf_op jit(solution)/shard_map/pallas_call | solution.py:431
  22.3 0.7 %copy.7 = f32[16,16,256]{2,1,0:T(8,128)} copy(f32[16,16,256]{2,1,0:T(8,128)S(1)} %shard_map.55) | data formatting | bytes 524288

commit v4 on v3

--- a/solution.py
+++ b/solution.py
@@ -40,6 +40,9 @@
     y_recv,
     factor_send,
     factor_recv,
+    local_send,
+    local_recv,
+    behind,
     gains,
     sum_send,
     sum_recv,
@@ -50,6 +53,8 @@
     y_recv_sem,
     factor_send_sem,
     factor_recv_sem,
+    local_send_sem,
+    local_recv_sem,
     sum_send_sem,
     sum_recv_sem,
 ):
@@ -109,10 +114,6 @@
     ends = (pz == 0, pz == nz - 1)
     below_count = (pz, nz - 1 - pz)
     for way in range(2):
-
-        @pl.when(ends[way])
-        def _():
-            factor_recv[way] = jnp.zeros(factor_recv.shape[1:], jnp.float32)
 
         for step in range(1, nz):
 
@@ -203,12 +204,22 @@
             device_id_type=MESH,
         )
 
-    def factor_copy(way, part):
+    def factor_copy(way, step):
         return pltpu.make_async_remote_copy(
-            src_ref=factor_send.at[way, part],
-            dst_ref=factor_recv.at[way, part],
-            send_sem=factor_send_sem.at[way, part],
-            recv_sem=factor_recv_sem.at[way, part],
+            src_ref=factor_send.at[way],
+            dst_ref=factor_recv.at[way],
+            send_sem=factor_send_sem.at[way, step - 1],
+            recv_sem=factor_recv_sem.at[way],
+            device_id={"gz": pz + step * (1 - 2 * way)},
+            device_id_type=MESH,
+        )
+
+    def local_copy(way):
+        return pltpu.make_async_remote_copy(
+            src_ref=local_send.at[way],
+            dst_ref=local_recv.at[way],
+            send_sem=local_send_sem.at[way],
+            recv_sem=local_recv_sem.at[way],
             device_id={"gz": pz + 1 - 2 * way},
             device_id_type=MESH,
         )
@@ -246,36 +257,66 @@
     own = (low_w.at[0], high_last)
     near_face, far_face = (face_first, face_last), (face_last, face_first)
 
+    ahead_count = (below_count[1], below_count[0])
+    odd = [lax.rem(below_count[way], 2) == 1 for way in range(2)]
+    skipped = []
+    for row in (base - depth, base + 2 * depth):
+        low = jnp.clip(row - 1, 0, total - 1)
+        high = jnp.clip(row, 0, total - 1)
+        width = jnp.full((8, LANES), spacing_at(low) + spacing_at(high), jnp.float32)
+        skipped.append(spread(coef_z * 2.0 / width))
+
     def pass_factor(way):
-        ratio = factor_recv[way, 0]
+        ratio = behind[way, 0]
         gain = first_both * near_face[way] / (1.0 - own[way][...] * near_face[way] * ratio)
         ahead = far_face[way] * (own[1 - way][...] + first_both * gain * ratio)
-
-        @pl.when(jnp.logical_not(ends[1 - way]))
+        scale = jnp.where(ends[way], 1.0, gain * behind[way, 1])
+
+        @pl.when(jnp.logical_not(odd[way]) & (ahead_count[way] >= 1))
         def _():
             factor_send[way, 0] = ahead
-            factor_copy(way, 0).start()
+            factor_send[way, 1] = scale
+
+            @pl.when(ahead_count[way] >= 2)
+            def _():
+                factor_copy(way, 2).start()
+
+            factor_copy(way, 1).start()
 
         gains[way, 0] = gain
         gains[way, 1] = gain * ratio
         gains[way, 2] = ahead
-
-    def pass_scale(way):
-        scale = jnp.where(ends[way], 1.0, gains[way, 0] * factor_recv[way, 1])
-
-        @pl.when(jnp.logical_not(ends[1 - way]))
-        def _():
-            factor_send[way, 1] = scale
-            factor_copy(way, 1).start()
-
         gains[way, 3] = 1.0 / scale
 
+    def take_factor(way):
+        @pl.when(odd[way])
+        def _():
+            factor_copy(way, 1).wait_recv()
+            behind[way] = factor_recv[way]
+
+        @pl.when(jnp.logical_not(odd[way]))
+        def _():
+            factor_copy(way, 2).wait_recv()
+            local_copy(way).wait_recv()
+            ratio = factor_recv[way, 0]
+            both = local_recv[way, 1]
+            gain = both * skipped[way] / (1.0 - local_recv[way, 0] * skipped[way] * ratio)
+            behind[way, 0] = near_face[way] * (local_recv[way, 2] + both * gain * ratio)
+            behind[way, 1] = gain * factor_recv[way, 1]
+
     for way in range(2):
 
         @pl.when(ends[way])
         def _():
+            behind[way] = jnp.zeros(behind.shape[1:], jnp.float32)
             pass_factor(way)
-            pass_scale(way)
+
+        @pl.when(odd[way] & (ahead_count[way] >= 1))
+        def _():
+            local_send[way, 0] = own[way][...]
+            local_send[way, 1] = first_both
+            local_send[way, 2] = own[1 - way][...]
+            local_copy(way).start()
 
     loads[2].wait()
     loads[3].wait()
@@ -340,10 +381,8 @@
         def advance(way):
             @pl.when(jnp.logical_not(ends[way]))
             def _():
-                factor_copy(way, 0).wait_recv()
+                take_factor(way)
                 pass_factor(way)
-                factor_copy(way, 1).wait_recv()
-                pass_scale(way)
 
             send_sums(way)
 
@@ -376,9 +415,9 @@
             value = sum_recv[turn, way, 0]
             for step in range(2, nz):
                 value = value + sum_recv[turn, way, step - 1]
-            arrived.append(factor_recv[way, 1] * value)
+            arrived.append(behind[way, 1] * value)
         below, above = arrived
-        up_ratio, down_ratio = factor_recv[0, 0], factor_recv[1, 0]
+        up_ratio, down_ratio = behind[0, 0], behind[1, 0]
         up_next = gains[0, 2]
         carried = gains[0, 0] * below + gains[0, 1] * first_value + last_value
         last_cell = (carried + up_next * above) / (1.0 - up_next * down_ratio)
@@ -407,10 +446,15 @@
         on_sides(py, ny, lambda side: y_copy(turn, side).wait_send())
     for way in range(2):
 
-        @pl.when(jnp.logical_not(ends[1 - way]))
-        def _():
-            factor_copy(way, 0).wait_send()
-            factor_copy(way, 1).wait_send()
+        @pl.when(odd[way] & (ahead_count[way] >= 1))
+        def _():
+            local_copy(way).wait_send()
+
+        for step in (1, 2):
+
+            @pl.when(jnp.logical_not(odd[way]) & (ahead_count[way] >= step))
+            def _():
+                factor_copy(way, step).wait_send()
 
         for step in range(1, nz):
 
@@ -450,6 +494,9 @@
             pltpu.VMEM((2, 2, depth, wide_x, LANES), f32),
             pltpu.VMEM((2, 2) + plane, f32),
             pltpu.VMEM((2, 2) + plane, f32),
+            pltpu.VMEM((2, 3) + plane, f32),
+            pltpu.VMEM((2, 3) + plane, f32),
+            pltpu.VMEM((2, 2) + plane, f32),
             pltpu.VMEM((2, 4) + plane, f32),
             pltpu.VMEM((2, 2) + plane, f32),
             pltpu.VMEM((2, 2, others) + plane, f32),
@@ -459,7 +506,9 @@
             dma((2, 2)),
             dma((2, 2)),
             dma((2, 2)),
-            dma((2, 2)),
+            dma((2,)),
+            dma((2,)),
+            dma((2,)),
             dma((2, 2, others)),
             dma((2, 2, others)),
         ],

time: 23.1 us -> 21.4 us (0.926)
  Pallas kernels: 22.2 us -> 20.5 us
    pallas_call x1, Pallas kernels: 22.2 us -> 20.5 us  [on_device(): pl.pallas_call(functools.partial(relax_kernel, counts), out_shape=pltpu.V...]
where the time goes in v4:
time: 21.4 us; the launch traced here: 21.3 us
  Pallas kernels  20.5 us (96%)
  local copies, waits for them, and re-layouts  0.71 us (3%)
    pallas_call x1, Pallas kernels, on_device(): pl.pallas_call(functools.partial(relax_kernel, counts), out_shape=pltpu.V...  20.5 us
    unnamed x1, local copies, waits for them, and re-layouts  0.71 us

profile of v4, /device:TPU:0, one launch (start us, length us, event | category | flops | bytes accessed | tf_op | source)
XLA Modules:
  0.0 21.3 jit_solution(15398134704201853228)
XLA Ops:
  0.0 20.5 %shard_map.55 = f32[16,16,256]{2,1,0:T(8,128)S(1)} custom-call(s32[64]{0:T(128)} %level_ref.1, f32[16,16,256]{2,1,0:T(8,128)} %corr_hbm.1, f32[16,16,256]{2,1,0:T(8,128)} %res_hbm.1, f32[16,16,256]{2,1,0:T(8,128)} %state_hbm.1, s32[16,256]{1,0:T(8,128)} %colour_hbm.1), custom_call_target="tpu_custom_call" | custom-call | tf_op jit(solution)/shard_map/pallas_call | solution.py:475
  20.5 0.7 %copy.7 = f32[16,16,256]{2,1,0:T(8,128)} copy(f32[16,16,256]{2,1,0:T(8,128)S(1)} %shard_map.55) | data formatting | bytes 524288
